TPU v7x, 256 devices: a whole 4x4x8 slice. The times are simulated.
256 devices in a mesh: seq: 32 (over y_lo, z, core), tp: 8 (over x, y_hi).
Axes of the slice: x: 4, y: 4 (y_hi: 2, y_lo: 2; y = y_hi * 2 + y_lo), z: 8, core: 2. Of those that a mesh axis runs over, the one named last changes fastest.
Arguments:
- query: bfloat16 [6144, 5120], P('seq', 'tp')
- span_keys: bfloat16 [6144, 5120], P('seq', 'tp'), may hold values from -6 to 6
- span_values: bfloat16 [6144, 5120], P('seq', 'tp'), may hold values from -48 to 48
- cache_keys: bfloat16 [8, 8192, 5120], P(None, 'seq', 'tp'), may hold values from -6 to 6
- cache_values: bfloat16 [8, 8192, 5120], P(None, 'seq', 'tp'), may hold values from -48 to 48
- out_weight: bfloat16 [5120, 5120], P('tp'), may hold values from -0.078125 to 0.078125
- cache_lengths: int32 [8], replicated, may hold values from 1 to 8192, as said below
- sink_counts: int32 [8], replicated, may hold values from 1 to 256, as said below
- windows: int32 [8], replicated, may hold values from 2048 to 4096, as said below
- block_of_slot: int32 [8, 32], replicated, may hold values from 0 to 31, each once within a row
Outputs:
- projected: bfloat16 [6144, 5120], P('seq', 'tp')
Inputs may be any that keep to these rules, and one draw needn't show every extreme that they name: `cache_lengths`: at least 1 and at most 8192; some request has exactly 8192. `sink_counts`: some request has exactly 256. `windows`: some request has exactly 4096. `block_of_slot`: each row is a permutation of 0 to 31.
All inputs are finite; a program needn't handle non-finite values.
Results may differ from a plain program's by a relative error of at most 0.015.
Values may be sent and summed in bfloat16 or wider, within the bound.
A program may use at most 192 MiB of HBM per device.

v0:
```python
import math
import jax
import jax.numpy as jnp
import numpy as np
from jax import lax
from jax.sharding import Mesh
from jax.sharding import PartitionSpec as P

HEAD = 128
GROUP = 4
NEG = -1e30


def visible(query_pos, key_pos, valid, window, sinks):
    later = query_pos[:, None]
    earlier = key_pos[None, :]
    near = later - earlier < window
    return (earlier <= later) & (near | (earlier < sinks)) & valid[None, :]


def block_partial(q_rows, keys, vals, query_pos, key_pos, valid, window, sinks):
    mask = visible(query_pos, key_pos, valid, window, sinks)
    scale = 1.0 / math.sqrt(q_rows.shape[-1])
    scores = jnp.einsum("qhd,khd->hqk", q_rows, keys, preferred_element_type=jnp.float32) * scale
    scores = jnp.where(mask[None], scores, NEG)
    top = jnp.max(scores, axis=2)
    weights = jnp.where(mask[None], jnp.exp(scores - top[:, :, None]), 0.0)
    total = jnp.sum(weights, axis=2)
    summed = jnp.einsum(
        "hqk,khd->qhd", weights.astype(jnp.bfloat16), vals, preferred_element_type=jnp.float32
    )
    return (summed, top.T, total.T)


def shards(
    query,
    span_keys,
    span_values,
    cache_keys,
    cache_values,
    out_weight,
    cache_lengths,
    sink_counts,
    windows,
    block_of_slot,
):
    rows, width = query.shape
    heads_here = width // HEAD
    places = lax.axis_size("place")
    group = lax.axis_size("req")
    place = lax.axis_index("place")
    mine = lax.axis_index("req")
    cache_dev = cache_keys.shape[1]
    length = cache_lengths[mine]
    window = windows[mine]
    sinks = sink_counts[mine]
    got_keys = lax.all_to_all(cache_keys, "req", split_axis=0, concat_axis=0, tiled=True)
    got_vals = lax.all_to_all(cache_values, "req", split_axis=0, concat_axis=0, tiled=True)
    span_q = lax.all_gather(query, "place", axis=0, tiled=True)
    blocks = lax.dynamic_slice_in_dim(block_of_slot[mine], place * group, group)
    slot_pos = (
        blocks[:, None] * cache_dev + jnp.arange(cache_dev, dtype=jnp.int32)[None, :]
    ).reshape(-1)
    own_pos = length + place * rows + jnp.arange(rows, dtype=jnp.int32)
    query_pos = length + jnp.arange(places * rows, dtype=jnp.int32)
    keys = jnp.concatenate([got_keys.reshape(-1, width), span_keys], 0).reshape(
        -1, heads_here, HEAD
    )
    vals = jnp.concatenate([got_vals.reshape(-1, width), span_values], 0).reshape(
        -1, heads_here, HEAD
    )
    key_pos = jnp.concatenate([slot_pos, own_pos])
    valid = jnp.concatenate([slot_pos < length, jnp.ones((rows,), jnp.bool_)])
    summed, top, total = block_partial(
        span_q.reshape(-1, heads_here, HEAD), keys, vals, query_pos, key_pos, valid, window, sinks
    )
    summed = lax.all_to_all(
        summed.reshape(places, rows, width), "place", split_axis=0, concat_axis=0, tiled=True
    ).reshape(places, rows, heads_here, HEAD)
    stats = jnp.concatenate([top, total], axis=1).reshape(places, rows, 2 * heads_here)
    stats = lax.all_to_all(stats, "place", split_axis=0, concat_axis=0, tiled=True)
    top, total = (stats[..., :heads_here], stats[..., heads_here:])
    best = jnp.max(top, axis=0)
    factor = jnp.exp(top - best[None])
    total = jnp.sum(total * factor, axis=0)
    summed = jnp.sum(summed * factor[..., None], axis=0)
    attention = (summed / total[..., None]).astype(jnp.bfloat16).reshape(rows, width)
    terms = jnp.dot(attention, out_weight, preferred_element_type=jnp.float32)
    return lax.psum_scatter(terms.astype(jnp.bfloat16), "tp", scatter_dimension=1, tiled=True)


def solution(mesh):
    seq_size = mesh.shape["seq"]
    requests = 8
    grid = Mesh(
        np.asarray(mesh.devices).reshape(seq_size // requests, requests, mesh.shape["tp"]),
        ("place", "req", "tp"),
    )
    seq = ("place", "req")
    return jax.shard_map(
        shards,
        mesh=grid,
        in_specs=(
            P(seq, "tp"),
            P(seq, "tp"),
            P(seq, "tp"),
            P(None, seq, "tp"),
            P(None, seq, "tp"),
            P("tp", None),
            P(),
            P(),
            P(),
            P(),
        ),
        out_specs=P(seq, "tp"),
        check_vma=False,
    )
```

profile of v0, /device:TPU:2, one launch (start us, length us, event | category | flops | bytes accessed | tf_op | source)
XLA Modules:
  0.0 391.5 jit_solution(4118115496891298422)
XLA Ops:
  6.5 66.3 %all_to_all.20 = bf16[8,256,640]{2,1,0:T(8,128)(2,1)} all-to-all(bf16[8,256,640]{2,1,0:T(8,128)(2,1)} %param.14), channel_id=1, replica_groups=mesh['place'=4,'req'=8,'tp'=8] {'req'}, dimensions={0} | all-to-all | bytes 5242880 | tf_op jit(solution)/shard_map/all_to_all | solution.py:58
  72.8 0.0 copy-start.5
  72.8 0.0 copy-start.6
  72.8 0.0 copy-start.7
  72.8 0.0 copy-start.3
  72.8 0.0 copy-start.2
  72.8 3.8 all-to-all-start.1
  76.6 0.0 copy-done.5
  76.6 0.7 dynamic_slice.15
  77.3 0.0 copy-done.6
  77.3 0.6 dynamic_slice.16
  77.9 0.0 copy-done.7
  77.9 0.7 dynamic_slice.14
  78.5 0.8 multiply_bitcast_fusion
  79.3 0.1 add_bitcast_fusion
  79.4 0.0 copy-done.3
  79.4 0.2 copy.38
  79.6 0.9 copy.40
  80.4 1.1 copy.34
  81.6 0.2 copy.36
  81.8 0.0 copy-done.2
  81.8 77.9 %all_gather.3 = bf16[768,640]{1,0:T(8,128)(2,1)} all-gather(bf16[192,640]{1,0:T(8,128)(2,1)S(1)} %copy-done.2), channel_id=1, replica_groups=mesh['place'=4,'req'=8,'tp'=8] {'place'}, dimensions={0}, use_global_device_ids=true | all-gather | bytes 1228800 | tf_op jit(solution)/shard_map/all_gather | solution.py:59
  159.7 2.3 copy.41
  162.6 0.7 broadcast_compare_fusion.1
  163.3 0.6 broadcast_compare_fusion
  163.9 0.7 iota_add_fusion
  164.6 4.6 %fusion.7 = pred[768,2240]{0,1:T(8,128)(4,1)} fusion(s32[]{:T(128)} %bitcast.3, s32[768]{0:T(1024)S(1)} %iota_add_fusion, s32[2240]{0:T(1024)S(1)} %pad_add_fusion, pred[2240]{0:T(1024)(128)(4,1)S(1)} %concatenate.33, pred[2240]{0:T(1024)(128)(4,1)S(1)} %broadcast_compare_fusion), kind=kLoop, calls=%fused_computation.9 | loop fusion | flops 10321920 | bytes 1736836 | tf_op jit(solution)/shard_map/and | solution.py:18
  169.2 7.0 %reshape.156 = bf16[2048,5,128]{2,1,0:T(8,128)(2,1)} reshape(bf16[8,256,640]{2,1,0:T(8,128)(2,1)} %all_to_all.20) | data formatting | bytes 5242880 | tf_op jit(solution)/shard_map/concatenate | solution.py:69
  176.2 4.0 %copy.35 = bf16[2048,5,128]{2,0,1:T(8,128)(2,1)} copy(bf16[2048,5,128]{2,1,0:T(8,128)(2,1)} %reshape.156) | data formatting | bytes 5242880 | tf_op jit(solution)/shard_map/concatenate | solution.py:69
  180.3 0.0 all-to-all-done.1
  180.3 4.2 %reshape.157 = bf16[2048,5,128]{2,1,0:T(8,128)(2,1)} reshape(bf16[8,256,640]{2,1,0:T(8,128)(2,1)S(1)} %all-to-all-done.1) | data formatting | bytes 5242880 | tf_op jit(solution)/shard_map/concatenate | solution.py:66
  184.5 0.0 copy-start
  184.5 0.0 copy-start.1
  184.5 0.0 copy-start.4
  184.5 2.7 copy.39
  187.2 0.0 copy-done
  187.2 0.3 copy-done.1
  187.4 0.0 copy-done.4
  187.5 13.8 %fusion.25 = (f32[5,768]{1,0:T(8,128)S(1)}, f32[5,768,2240]{1,2,0:T(8,128)}) fusion(bf16[768,5,128]{0,2,1:T(8,128)(2,1)S(1)} %bitcast.41, bf16[192,5,128]{2,0,1:T(8,128)(2,1)S(1)} %copy-done.4, bf16[2048,5,128]{2,0,1:T(8,128)(2,1)S(1)} %copy.39, pred[768,2240]{0,1:T(8,128)(4,1)S(1)} %copy-done), kind=kOutput, calls=%fused_computation.37 | convolution fusion | flops 2233544960 | bytes 39992320 | tf_op jit(solution)/shard_map/qhd,khd->hqk/dot_general | solution.py:24
  201.3 14.2 %fusion = f32[5,768]{1,0:T(8,128)S(1)} fusion(f32[5,768,2240]{1,2,0:T(8,128)} %get-tuple-element.8, f32[5,768]{1,0:T(8,128)S(1)} %get-tuple-element.7, pred[768,2240]{0,1:T(8,128)(4,1)S(1)} %copy-done), kind=kLoop, calls=%fused_computation.2 | loop fusion | flops 25800960 | bytes 36157440 | tf_op jit(solution)/shard_map/reduce_sum | solution.py:28
  215.5 0.1 reshape.155
  215.6 0.7 reshape.160
  216.3 3.8 all-to-all-start.3
  220.1 16.6 %fusion.15 = f32[768,5,128]{0,2,1:T(8,128)} fusion(f32[5,768,2240]{1,2,0:T(8,128)} %get-tuple-element.8, f32[5,768]{1,0:T(8,128)S(1)} %get-tuple-element.7, pred[768,2240]{0,1:T(8,128)(4,1)S(1)} %copy-done, bf16[192,5,128]{2,0,1:T(8,128)(2,1)S(1)} %copy.36, bf16[2048,5,128]{2,0,1:T(8,128)(2,1)} %copy.35), kind=kOutput, calls=%fused_computation.19 | convolution fusion | flops 2233548800 | bytes 40975360 | tf_op jit(solution)/shard_map/hqk,khd->qhd/dot_general | solution.py:29
  236.7 3.1 reshape.154
  239.8 2.5 copy.43
  242.4 0.0 all-to-all-done.3
  242.4 8.1 %all-to-all-start.2 = ((f32[4,192,640]{2,1,0:T(8,128)}), f32[4,192,640]{2,1,0:T(8,128)}, u32[]{:S(2)}, u32[]{:S(2)}) async-start(f32[4,192,640]{2,1,0:T(8,128)} %copy.43), calls=%async_computation.2 | async-start | bytes 3932160 | tf_op jit(solution)/shard_map/all_to_all | solution.py:77
  250.5 0.0 reduce-scatter.4.cloned.1.call-start
  250.5 0.5 broadcast.100
  251.0 0.7 reduce.1
  251.7 0.1 reshape.161
  251.8 35.7 %all-to-all-done.2 = f32[4,192,640]{2,1,0:T(8,128)} async-done(((f32[4,192,640]{2,1,0:T(8,128)}), f32[4,192,640]{2,1,0:T(8,128)}, u32[]{:S(2)}, u32[]{:S(2)}) %all-to-all-start.2) | async-done | bytes 1966112 | tf_op jit(solution)/shard_map/all_to_all | solution.py:77
  287.5 2.0 copy.45
  289.6 0.2 fusion.14
  289.8 0.1 fusion.20
  289.9 4.6 %convolution_convert_fusion = bf16[192,5120]{1,0:T(8,128)(2,1)S(1)} fusion(bf16[192,640]{0,1:T(8,128)(2,1)S(1)} %fusion.20, bf16[640,5120]{1,0:T(8,128)(2,1)} %param.15), kind=kOutput, calls=%fused_computation.10 | convolution fusion | flops 1259274240 | bytes 8765440 | tf_op jit(solution)/shard_map/dot_general | solution.py:88
  294.5 2.6 copy.51
  297.0 0.0 reduce-scatter.4.cloned.1.call-update
  297.1 85.7 %reduce-scatter.4.cloned.1.call-done = bf16[640,192]{1,0:T(8,128)(2,1)} async-done(((bf16[5120,192]{1,0:T(8,128)(2,1)}), bf16[640,192]{1,0:T(8,128)(2,1)}) %reduce-scatter.4.cloned.1.call-update) | async-done | bytes 245776
  382.8 1.8 copy.52
  (8 shorter events, 0.1 us)
Async XLA Ops:
  72.8 3.8 copy-start.5
  72.8 4.5 %copy-start.6 = (s32[8]{0:T(128)S(1)}, s32[8]{0:T(128)}, u32[]{:S(2)}) copy-start(s32[8]{0:T(128)} %param.17) | copy-start | bytes 100
  72.8 5.1 %copy-start.7 = (s32[8]{0:T(128)S(1)}, s32[8]{0:T(128)}, u32[]{:S(2)}) copy-start(s32[8]{0:T(128)} %param.16) | copy-start | bytes 100
  72.8 6.6 %copy-start.3 = (bf16[192,640]{1,0:T(8,128)(2,1)S(1)}, bf16[192,640]{1,0:T(8,128)(2,1)}, u32[]{:S(2)}) copy-start(bf16[192,640]{1,0:T(8,128)(2,1)} %param.11) | copy-start | bytes 737284
  72.8 8.9 %copy-start.2 = (bf16[192,640]{1,0:T(8,128)(2,1)S(1)}, bf16[192,640]{1,0:T(8,128)(2,1)}, u32[]{:S(2)}) copy-start(bf16[192,640]{1,0:T(8,128)(2,1)} %param.10) | copy-start | bytes 737284
  72.8 107.4 %all-to-all-start.1 = ((bf16[8,256,640]{2,1,0:T(8,128)(2,1)}), bf16[8,256,640]{2,1,0:T(8,128)(2,1)S(1)}, u32[]{:S(2)}, u32[]{:S(2)}) async-start(bf16[8,256,640]{2,1,0:T(8,128)(2,1)} %param.13), calls=%async_computation.1 | async-start | bytes 5242880 | tf_op jit(solution)/shard_map/all_to_all | solution.py:57
  184.5 2.7 copy-start
  184.5 3.0 copy-start.1
  184.5 3.0 copy-start.4
  216.3 26.1 %all-to-all-start.3 = ((f32[4,1,1920]{2,1,0:T(1,128)}), f32[4,1,1920]{2,1,0:T(1,128)S(1)}, u32[]{:S(2)}, u32[]{:S(2)}) async-start(f32[4,1,1920]{2,1,0:T(1,128)} %reshape.160), calls=%async_computation.3 | async-start | bytes 61440 | tf_op jit(solution)/shard_map/all_to_all | solution.py:81
  242.4 45.2 %all-to-all-start.2 = ((f32[4,192,640]{2,1,0:T(8,128)}), f32[4,192,640]{2,1,0:T(8,128)}, u32[]{:S(2)}, u32[]{:S(2)}) async-start(f32[4,192,640]{2,1,0:T(8,128)} %copy.43), calls=%async_computation.2 | async-start | bytes 3932160 | tf_op jit(solution)/shard_map/all_to_all | solution.py:77
  250.5 132.3 %reduce-scatter.4.cloned.1.call-start = ((), (), s32[]{:S(2)}) async-start(), calls=%async_computation.5 | async-start | bytes 2949120
Sparse Core Ops, SparseCore 0:
  297.2 85.5 reduce-scatter.3
where the time goes:
time: 392 us; the launch traced here: 391 us
  blocking collectives  144 us (37%)
  waiting for transfers between devices  121 us (31%)
  local copies, waits for them, and re-layouts  38.3 us (10%)
  matrix products  35 us (9%)
  other arithmetic  22.6 us (6%)
  starting transfers between devices  15.7 us (4%)
  between operations  14.3 us (4%)
    unnamed x2, waiting for transfers between devices  85.7 us
    all_gather x1, blocking collectives, shards(): span_q = lax.all_gather(query, 'place', axis=0, tiled=True)  77.9 us
    all_to_all x1, blocking collectives, shards(): lax.all_to_all(cache_values, 'req', split_axis=0, concat_axis=0, tiled=True)  66.3 us
    all_to_all x1, waiting for transfers between devices, shards(): lax.all_to_all(summed.reshape(places, rows, width), 'place', split_axis=0...  35.7 us
    dot_general x1, matrix products, block_partial(): jnp.einsum('hqk,khd->qhd', weights.astype(jnp.bfloat16), vals, preferred_...  16.6 us
    reduce_sum x1, other arithmetic, block_partial(): total = jnp.sum(weights, axis=2)  14.2 us
    dot_general x1, matrix products, block_partial(): jnp.einsum('qhd,khd->hqk', q_rows, keys, preferred_element_type=jnp.float32)  13.8 us
    concatenate x3, local copies, waits for them, and re-layouts, shards(): jnp.concatenate([got_vals.reshape(-1, width), span_values], 0)  11.2 us
  transfers between devices with their start and end apart: 4, of which 2 were waited for; matrix products, arithmetic and copies ran while one was open for 12% of the time, Pallas kernels for 0%

commit v1 on v0

--- a/solution.py
+++ b/solution.py
@@ -56,7 +56,9 @@
     sinks = sink_counts[mine]
     got_keys = lax.all_to_all(cache_keys, "req", split_axis=0, concat_axis=0, tiled=True)
     got_vals = lax.all_to_all(cache_values, "req", split_axis=0, concat_axis=0, tiled=True)
-    span_q = lax.all_gather(query, "place", axis=0, tiled=True)
+    span_q = jnp.concatenate(
+        lax.all_to_all(jnp.stack([query] * lax.axis_size("place")), "place", 0, 0), axis=0
+    )
     blocks = lax.dynamic_slice_in_dim(block_of_slot[mine], place * group, group)
     slot_pos = (
         blocks[:, None] * cache_dev + jnp.arange(cache_dev, dtype=jnp.int32)[None, :]

time: 392 us -> 365 us (0.931)
  blocking collectives: 144 us -> 35.7 us
  waiting for transfers between devices: 121 us -> 196 us
  starting transfers between devices: 15.7 us -> 20.4 us
    all_gather x1 -> x0, blocking collectives: 77.9 us -> none  [shards(): span_q = lax.all_gather(query, 'place', axis=0, tiled=True)]
    all_to_all x1, waiting for transfers between devices: 0.01 us -> 53.4 us  [shards(): lax.all_to_all(cache_keys, 'req', split_axis=0, concat_axis=0, tiled=True)]
    all_to_all x1, blocking collectives: 66.3 us -> 35.7 us  [shards(): lax.all_to_all(jnp.stack([query] * lax.axis_size('place')), 'place', 0, 0)]
    all_to_all x0 -> x1, waiting for transfers between devices: none -> 15.5 us  [shards(): lax.all_to_all(cache_values, 'req', split_axis=0, concat_axis=0, tiled=True)]
    all_to_all x1, waiting for transfers between devices: 35.7 us -> 44.1 us  [shards(): lax.all_to_all(summed.reshape(places, rows, width), 'place', split_axis=0...]
    another operation x0 -> x2, local copies, waits for them, and re-layouts: none -> 4.52 us  [the longest x1 3.5 us: shards(): span_q.reshape(-1, heads_here, HEAD)]
    all_to_all x0 -> x1, starting transfers between devices: none -> 4.42 us  [shards(): lax.all_to_all(cache_values, 'req', split_axis=0, concat_axis=0, tiled=True)]
  transfers between devices with their start and end apart: 4 -> 5, of which waited for: 2 -> 4; matrix products, arithmetic and copies ran while one was open for 12% -> 23% of each run, Pallas kernels for 0% -> 0%
where the time goes in v1:
time: 365 us; the launch traced here: 364 us
  waiting for transfers between devices  196 us (54%)
  local copies, waits for them, and re-layouts  39.8 us (11%)
  blocking collectives  35.7 us (10%)
  matrix products  35.4 us (10%)
  other arithmetic  22.7 us (6%)
  starting transfers between devices  20.4 us (6%)
  between operations  14.3 us (4%)
    unnamed x2, waiting for transfers between devices  83.3 us
    all_to_all x1, waiting for transfers between devices, shards(): lax.all_to_all(cache_keys, 'req', split_axis=0, concat_axis=0, tiled=True)  53.4 us
    all_to_all x1, waiting for transfers between devices, shards(): lax.all_to_all(summed.reshape(places, rows, width), 'place', split_axis=0...  44.1 us
    all_to_all x1, blocking collectives, shards(): lax.all_to_all(jnp.stack([query] * lax.axis_size('place')), 'place', 0, 0)  35.7 us
    dot_general x1, matrix products, block_partial(): jnp.einsum('hqk,khd->qhd', weights.astype(jnp.bfloat16), vals, preferred_...  16.6 us
    all_to_all x1, waiting for transfers between devices, shards(): lax.all_to_all(cache_values, 'req', split_axis=0, concat_axis=0, tiled=True)  15.5 us
    dot_general x1, matrix products, block_partial(): jnp.einsum('qhd,khd->hqk', q_rows, keys, preferred_element_type=jnp.float32)  14.3 us
    reduce_sum x1, other arithmetic, block_partial(): total = jnp.sum(weights, axis=2)  14.2 us
  transfers between devices with their start and end apart: 5, of which 4 were waited for; matrix products, arithmetic and copies ran while one was open for 23% of the time, Pallas kernels for 0%

profile of v1, /device:TPU:2, one launch (start us, length us, event | category | flops | bytes accessed | tf_op | source)
XLA Modules:
  0.0 364.4 jit_solution(187640124922260332)
XLA Ops:
  6.5 1.0 stack.2
  7.6 35.7 %all_to_all.25 = bf16[4,192,640]{2,1,0:T(8,128)(2,1)} all-to-all(bf16[4,192,640]{2,1,0:T(8,128)(2,1)S(1)} %stack.2), channel_id=1, replica_groups=mesh['place'=4,'req'=8,'tp'=8] {'place'}, dimensions={0} | all-to-all | bytes 1966080 | tf_op jit(solution)/shard_map/all_to_all | solution.py:60
  43.2 0.0 copy-start.7
  43.2 0.0 copy-start.8
  43.2 0.0 copy-start.9
  43.2 0.0 copy-start.2
  43.2 0.0 copy-start.3
  43.2 4.7 %all-to-all-start.1 = ((bf16[8,256,640]{2,1,0:T(8,128)(2,1)}), bf16[8,256,640]{2,1,0:T(8,128)(2,1)S(1)}, u32[]{:S(2)}, u32[]{:S(2)}) async-start(bf16[8,256,640]{2,1,0:T(8,128)(2,1)} %param.13), calls=%async_computation.1 | async-start | bytes 5242880 | tf_op jit(solution)/shard_map/all_to_all | solution.py:57
  47.9 0.8 multiply_bitcast_fusion
  48.7 0.1 add_bitcast_fusion
  48.7 0.0 copy-done.7
  48.8 0.7 dynamic_slice.14
  49.4 0.0 copy-done.8
  49.4 0.6 dynamic_slice.16
  50.0 0.0 copy-done.9
  50.0 0.7 dynamic_slice.15
  50.7 0.0 copy-done.2
  50.7 0.2 copy.38
  50.8 0.9 copy.40
  51.7 0.0 copy-done.3
  51.7 0.2 copy.34
  51.9 0.2 copy.36
  52.8 0.7 broadcast_compare_fusion.1
  53.5 0.6 broadcast_compare_fusion
  54.1 0.7 iota_add_fusion
  54.8 53.4 %all-to-all-done.1 = bf16[8,256,640]{2,1,0:T(8,128)(2,1)S(1)} async-done(((bf16[8,256,640]{2,1,0:T(8,128)(2,1)}), bf16[8,256,640]{2,1,0:T(8,128)(2,1)S(1)}, u32[]{:S(2)}, u32[]{:S(2)}) %all-to-all-start.1) | async-done | bytes 2621472 | tf_op jit(solution)/shard_map/all_to_all | solution.py:57
  108.2 4.4 %all-to-all-start = ((bf16[8,256,640]{2,1,0:T(8,128)(2,1)}), bf16[8,256,640]{2,1,0:T(8,128)(2,1)}, u32[]{:S(2)}, u32[]{:S(2)}) async-start(bf16[8,256,640]{2,1,0:T(8,128)(2,1)} %param.14), calls=%async_computation | async-start | bytes 5242880 | tf_op jit(solution)/shard_map/all_to_all | solution.py:58
  112.6 4.6 %fusion.7 = pred[768,2240]{0,1:T(8,128)(4,1)} fusion(s32[]{:T(128)} %bitcast.3, s32[768]{0:T(1024)S(1)} %iota_add_fusion, s32[2240]{0:T(1024)S(1)} %pad_add_fusion, pred[2240]{0:T(1024)(128)(4,1)S(1)} %concatenate.33, pred[2240]{0:T(1024)(128)(4,1)S(1)} %broadcast_compare_fusion), kind=kLoop, calls=%fused_computation.9 | loop fusion | flops 10321920 | bytes 1736836 | tf_op jit(solution)/shard_map/and | solution.py:18
  117.2 3.5 reshape.156
  120.7 4.2 %reshape.155 = bf16[2048,5,128]{2,1,0:T(8,128)(2,1)} reshape(bf16[8,256,640]{2,1,0:T(8,128)(2,1)S(1)} %all-to-all-done.1) | data formatting | bytes 5242880 | tf_op jit(solution)/shard_map/concatenate | solution.py:68
  124.9 0.0 copy-start
  124.9 0.0 copy-start.1
  124.9 2.7 copy.39
  127.6 0.0 copy-done
  127.6 0.5 copy-done.1
  128.1 0.0 copy-done.4
  128.1 14.3 %fusion.26 = (f32[5,768]{1,0:T(8,128)S(1)}, f32[5,768,2240]{1,2,0:T(8,128)}) fusion(bf16[768,5,128]{2,1,0:T(8,128)(2,1)S(1)} %copy-done.1, bf16[192,5,128]{2,0,1:T(8,128)(2,1)S(1)} %copy-done.4, bf16[2048,5,128]{2,0,1:T(8,128)(2,1)S(1)} %copy.39, pred[768,2240]{0,1:T(8,128)(4,1)S(1)} %copy-done), kind=kOutput, calls=%fused_computation.38 | convolution fusion | flops 2233544960 | bytes 39992320 | tf_op jit(solution)/shard_map/qhd,khd->hqk/dot_general | solution.py:24
  142.4 14.2 %fusion = f32[5,768]{1,0:T(8,128)S(1)} fusion(f32[5,768,2240]{1,2,0:T(8,128)} %get-tuple-element.8, f32[5,768]{1,0:T(8,128)S(1)} %get-tuple-element.7, pred[768,2240]{0,1:T(8,128)(4,1)S(1)} %copy-done), kind=kLoop, calls=%fused_computation.2 | loop fusion | flops 25800960 | bytes 36157440 | tf_op jit(solution)/shard_map/reduce_sum | solution.py:28
  156.6 0.0 copy-done.5
  156.6 0.1 reshape.153
  156.7 0.7 reshape.159
  157.4 15.5 %all-to-all-done = bf16[8,256,640]{2,1,0:T(8,128)(2,1)} async-done(((bf16[8,256,640]{2,1,0:T(8,128)(2,1)}), bf16[8,256,640]{2,1,0:T(8,128)(2,1)}, u32[]{:S(2)}, u32[]{:S(2)}) %all-to-all-start) | async-done | bytes 2621472 | tf_op jit(solution)/shard_map/all_to_all | solution.py:58
  172.9 3.4 all-to-all-start.4
  176.3 7.0 %reshape.154 = bf16[2048,5,128]{2,1,0:T(8,128)(2,1)} reshape(bf16[8,256,640]{2,1,0:T(8,128)(2,1)} %all-to-all-done) | data formatting | bytes 5242880 | tf_op jit(solution)/shard_map/concatenate | solution.py:71
  183.3 4.0 %copy.35 = bf16[2048,5,128]{2,0,1:T(8,128)(2,1)} copy(bf16[2048,5,128]{2,1,0:T(8,128)(2,1)} %reshape.154) | data formatting | bytes 5242880 | tf_op jit(solution)/shard_map/concatenate | solution.py:71
  187.4 0.0 copy-done.6
  187.4 16.6 %fusion.15 = f32[768,5,128]{0,2,1:T(8,128)} fusion(f32[5,768,2240]{1,2,0:T(8,128)} %get-tuple-element.8, f32[5,768]{1,0:T(8,128)S(1)} %copy-done.6, pred[768,2240]{0,1:T(8,128)(4,1)S(1)} %copy-done, bf16[192,5,128]{2,0,1:T(8,128)(2,1)S(1)} %copy.36, bf16[2048,5,128]{2,0,1:T(8,128)(2,1)} %copy.35), kind=kOutput, calls=%fused_computation.19 | convolution fusion | flops 2233548800 | bytes 40975360 | tf_op jit(solution)/shard_map/hqk,khd->qhd/dot_general | solution.py:29
  203.9 3.1 reshape.152
  207.1 2.6 copy.43
  209.6 0.0 all-to-all-done.4
  209.6 7.9 %all-to-all-start.3 = ((f32[4,192,640]{2,1,0:T(8,128)}), f32[4,192,640]{2,1,0:T(8,128)}, u32[]{:S(2)}, u32[]{:S(2)}) async-start(f32[4,192,640]{2,1,0:T(8,128)} %copy.43), calls=%async_computation.3 | async-start | bytes 3932160 | tf_op jit(solution)/shard_map/all_to_all | solution.py:79
  217.5 0.0 reduce-scatter.4.cloned.1.call-start
  217.5 0.5 broadcast.102
  218.0 0.7 reduce.1
  218.7 0.1 reshape.160
  218.9 44.1 %all-to-all-done.3 = f32[4,192,640]{2,1,0:T(8,128)} async-done(((f32[4,192,640]{2,1,0:T(8,128)}), f32[4,192,640]{2,1,0:T(8,128)}, u32[]{:S(2)}, u32[]{:S(2)}) %all-to-all-start.3) | async-done | bytes 1966112 | tf_op jit(solution)/shard_map/all_to_all | solution.py:79
  262.9 2.0 copy.45
  265.0 0.2 fusion.14
  265.2 0.1 fusion.21
  265.3 4.6 %convolution_convert_fusion = bf16[192,5120]{1,0:T(8,128)(2,1)S(1)} fusion(bf16[192,640]{0,1:T(8,128)(2,1)S(1)} %fusion.21, bf16[640,5120]{1,0:T(8,128)(2,1)} %param.15), kind=kOutput, calls=%fused_computation.10 | convolution fusion | flops 1259274240 | bytes 8765440 | tf_op jit(solution)/shard_map/dot_general | solution.py:90
  269.9 2.5 copy.54
  272.4 0.0 reduce-scatter.4.cloned.1.call-update
  272.4 83.3 %reduce-scatter.4.cloned.1.call-done = bf16[640,192]{1,0:T(8,128)(2,1)} async-done(((bf16[5120,192]{1,0:T(8,128)(2,1)}), bf16[640,192]{1,0:T(8,128)(2,1)}) %reduce-scatter.4.cloned.1.call-update) | async-done | bytes 245776
  355.7 1.8 copy.55
  (11 shorter events, 0.1 us)
Async XLA Ops:
  43.2 5.5 %copy-start.7 = (s32[8]{0:T(128)S(1)}, s32[8]{0:T(128)}, u32[]{:S(2)}) copy-start(s32[8]{0:T(128)} %param.16) | copy-start | bytes 100
  43.2 6.2 %copy-start.8 = (s32[8]{0:T(128)S(1)}, s32[8]{0:T(128)}, u32[]{:S(2)}) copy-start(s32[8]{0:T(128)} %param.17) | copy-start | bytes 100
  43.2 6.8 %copy-start.9 = (s32[8]{0:T(128)S(1)}, s32[8]{0:T(128)}, u32[]{:S(2)}) copy-start(s32[8]{0:T(128)} %param.18) | copy-start | bytes 100
  43.2 7.4 %copy-start.2 = (bf16[192,640]{1,0:T(8,128)(2,1)S(1)}, bf16[192,640]{1,0:T(8,128)(2,1)}, u32[]{:S(2)}) copy-start(bf16[192,640]{1,0:T(8,128)(2,1)} %param.11) | copy-start | bytes 737284
  43.2 8.5 %copy-start.3 = (bf16[192,640]{1,0:T(8,128)(2,1)S(1)}, bf16[192,640]{1,0:T(8,128)(2,1)}, u32[]{:S(2)}) copy-start(bf16[192,640]{1,0:T(8,128)(2,1)} %param.12) | copy-start | bytes 737284
  43.2 64.9 %all-to-all-start.1 = ((bf16[8,256,640]{2,1,0:T(8,128)(2,1)}), bf16[8,256,640]{2,1,0:T(8,128)(2,1)S(1)}, u32[]{:S(2)}, u32[]{:S(2)}) async-start(bf16[8,256,640]{2,1,0:T(8,128)(2,1)} %param.13), calls=%async_computation.1 | async-start | bytes 5242880 | tf_op jit(solution)/shard_map/all_to_all | solution.py:57
  108.2 64.7 %all-to-all-start = ((bf16[8,256,640]{2,1,0:T(8,128)(2,1)}), bf16[8,256,640]{2,1,0:T(8,128)(2,1)}, u32[]{:S(2)}, u32[]{:S(2)}) async-start(bf16[8,256,640]{2,1,0:T(8,128)(2,1)} %param.14), calls=%async_computation | async-start | bytes 5242880 | tf_op jit(solution)/shard_map/all_to_all | solution.py:58
  124.9 2.7 copy-start
  124.9 3.2 copy-start.1
  124.9 3.2 copy-start.4
  142.4 14.2 %copy-start.5 = (f32[5,768]{1,0:T(8,128)}, f32[5,768]{1,0:T(8,128)S(1)}, u32[]{:S(2)}) copy-start(f32[5,768]{1,0:T(8,128)S(1)} %get-tuple-element.7) | copy-start | bytes 46084
  172.9 36.7 %all-to-all-start.4 = ((f32[4,1,1920]{2,1,0:T(1,128)}), f32[4,1,1920]{2,1,0:T(1,128)S(1)}, u32[]{:S(2)}, u32[]{:S(2)}) async-start(f32[4,1,1920]{2,1,0:T(1,128)} %reshape.159), calls=%async_computation.4 | async-start | bytes 61440 | tf_op jit(solution)/shard_map/all_to_all | solution.py:83
  183.3 4.0 %copy-start.6 = (f32[5,768]{1,0:T(8,128)S(1)}, f32[5,768]{1,0:T(8,128)}, u32[]{:S(2)}) copy-start(f32[5,768]{1,0:T(8,128)} %copy-done.5) | copy-start | bytes 46084
  209.6 53.3 %all-to-all-start.3 = ((f32[4,192,640]{2,1,0:T(8,128)}), f32[4,192,640]{2,1,0:T(8,128)}, u32[]{:S(2)}, u32[]{:S(2)}) async-start(f32[4,192,640]{2,1,0:T(8,128)} %copy.43), calls=%async_computation.3 | async-start | bytes 3932160 | tf_op jit(solution)/shard_map/all_to_all | solution.py:79
  217.5 138.2 %reduce-scatter.4.cloned.1.call-start = ((), (), s32[]{:S(2)}) async-start(), calls=%async_computation.6 | async-start | bytes 2949120
Sparse Core Ops, SparseCore 0:
  272.6 83.1 reduce-scatter.3
